TPU v7x, 256 devices: a whole 4x4x8 slice. The times are simulated.
256 devices in a mesh: row: 8 (over z_hi, y), col: 32 (over x, z_lo, core).
Axes of the slice: x: 4, y: 4, z: 8 (z_hi: 2, z_lo: 4; z = z_hi * 4 + z_lo), core: 2. Of those that a mesh axis runs over, the one named last changes fastest.
Arguments:
- query_latent: bfloat16 [1024, 73728], P('row', 'col'), may hold values from -48 to 48
- kv_latent: bfloat16 [6144, 576], P('col'), may hold values from -6 to 6
- index_query: bfloat16 [1024, 8192], P('row'), may hold values from -18 to 18
- index_key: bfloat16 [6144, 128], P('col'), may hold values from -6 to 6
- head_weight: float32 [1024, 64], P('row'), may hold values from 0.05 to 0.5
- chosen: int32 [1024, 96], P('row'), may hold values from 0 to 1, as said below
- loss_grad: float32 [1024], P('row'), may hold values from 200 to 2000
Outputs:
- grad_query: float32 [1024, 8192], P('row', 'col')
- grad_key: float32 [6144, 128], P('col')
- grad_weight: float32 [1024, 64], P('row', 'col')
Inputs may be any that keep to these rules, and one draw needn't show every extreme that they name: `chosen`: each query t has exactly 32 ones, all in blocks at or before the block that holds its position 5120 + t, and that block is always among them.
All inputs are finite; a program needn't handle non-finite values.
Results may differ from a plain program's by a relative error of at most 0.0033.
Values may be sent and summed in bfloat16 or wider, within the bound.
No kernel may reach another device: no remote copies, remote signals or barrier semaphores. Data moves between devices by JAX's collectives and lax.ppermute only.
A program may use at most 64 MiB of HBM per device.

v0:
```python
import jax
import jax.numpy as jnp
from jax import lax
from jax.sharding import PartitionSpec as P

mla_scale = 192.0 ** (-0.5)
big_negative = -1e30


def body(query_latent, kv_latent, index_query, index_key, head_weight, chosen, loss_grad):
    row_count = lax.axis_size("row")
    col_count = lax.axis_size("col")
    row_index = lax.axis_index("row")
    col_index = lax.axis_index("col")
    rows_local = query_latent.shape[0]
    keys_local = kv_latent.shape[0]
    latent = kv_latent.shape[1]
    all_keys = keys_local * col_count
    all_queries = rows_local * row_count
    heads_local = query_latent.shape[1] // latent
    total_heads = heads_local * col_count
    block_count = chosen.shape[1]
    block_len = all_keys // block_count
    index_dim = index_key.shape[1]
    index_heads = index_query.shape[1] // index_dim
    heads_mine = index_heads // col_count
    inverse = index_dim ** (-0.5)
    query_pos = lax.iota(jnp.int32, rows_local) + row_index * rows_local + (all_keys - all_queries)
    key_pos = lax.iota(jnp.int32, all_keys)
    expand = jnp.broadcast_to(chosen[:, :, None], (rows_local, block_count, block_len)).reshape(
        rows_local, all_keys
    )
    allowed = (key_pos[None, :] <= query_pos[:, None]) & (expand > 0)
    keys_all = lax.all_gather(kv_latent, "col", axis=0, tiled=True)
    queries = query_latent.reshape(rows_local, heads_local, latent)
    summed = jnp.zeros((rows_local, all_keys), jnp.float32)
    for head_index in range(heads_local):
        scores = (
            jnp.einsum(
                "td,sd->ts", queries[:, head_index, :], keys_all, preferred_element_type=jnp.float32
            )
            * mla_scale
        )
        masked = jnp.where(allowed, scores, big_negative)
        highest = jnp.max(masked, axis=1, keepdims=True)
        raised = jnp.where(allowed, jnp.exp(masked - highest), 0.0)
        summed = summed + raised / jnp.sum(raised, axis=1, keepdims=True)
    target = lax.psum_scatter(summed, "col", scatter_dimension=1, tiled=True) / total_heads
    local_allowed = lax.dynamic_slice_in_dim(allowed, col_index * keys_local, keys_local, 1)
    index_rows = index_query.reshape(rows_local, index_heads, index_dim)
    affinity = (
        jnp.einsum("tjd,sd->tjs", index_rows, index_key, preferred_element_type=jnp.float32)
        * inverse
    )
    logits = jnp.sum(head_weight[:, :, None] * jax.nn.softplus(affinity), axis=1)
    masked = jnp.where(local_allowed, logits, big_negative)
    highest = lax.pmax(jnp.max(masked, axis=1), "col")
    raised = jnp.where(local_allowed, jnp.exp(masked - highest[:, None]), 0.0)
    total = lax.psum(jnp.sum(raised, axis=1), "col")
    chance = raised / total[:, None]
    grad_logit = jnp.where(local_allowed, loss_grad[:, None] * (chance - target), 0.0).astype(
        jnp.bfloat16
    )
    grad_wide = lax.optimization_barrier(grad_logit).astype(jnp.float32)
    slopes = (grad_wide[:, None, :] * jax.nn.sigmoid(affinity)).astype(jnp.bfloat16)
    weighted = (head_weight[:, :, None] * index_rows).astype(jnp.bfloat16)
    key_part = jnp.einsum("tjs,tjd->sd", slopes, weighted, preferred_element_type=jnp.float32)
    grad_key = lax.psum(key_part, "row") * inverse
    own_start = col_index * heads_mine
    own_weight = lax.dynamic_slice_in_dim(head_weight, own_start, heads_mine, 1)
    query_part = jnp.einsum(
        "tjs,sd->tjd", slopes, index_key, preferred_element_type=jnp.float32
    ).reshape(rows_local, index_heads * index_dim)
    weight_part = jnp.sum(grad_wide[:, None, :] * jax.nn.softplus(affinity), axis=2)
    query_flat, grad_weight = (
        lax.psum_scatter(query_part, "col", scatter_dimension=1, tiled=True),
        lax.psum_scatter(weight_part, "col", scatter_dimension=1, tiled=True),
    )
    query_sum = query_flat.reshape(rows_local, heads_mine, index_dim)
    grad_query = (query_sum * (own_weight * inverse)[:, :, None]).reshape(
        rows_local, heads_mine * index_dim
    )
    return (grad_query, grad_key, grad_weight)


def solution(mesh):
    in_specs = (
        P("row", "col"),
        P("col", None),
        P("row", None),
        P("col", None),
        P("row", None),
        P("row", None),
        P("row"),
    )
    out_specs = (P("row", "col"), P("col", None), P("row", "col"))
    return jax.shard_map(body, mesh=mesh, in_specs=in_specs, out_specs=out_specs, check_vma=False)
```

profile of v0, /device:TPU:16, one launch (start us, length us, event | category | flops | bytes accessed | tf_op | source)
XLA Modules:
  0.0 522.7 jit_solution(10032148616950255443)
XLA Ops:
  7.2 0.7 all-gather.2.cloned.1.call-update
  8.0 1.4 copy.32
  9.3 0.8 broadcast_compare_fusion
  10.2 0.6 fusion.4
  10.8 70.3 %all-gather.2.cloned.1.call-done = bf16[6144,576]{1,0:T(8,128)(2,1)} async-done(((bf16[192,576]{1,0:T(8,128)(2,1)}), bf16[6144,576]{1,0:T(8,128)(2,1)}) %all-gather.2.cloned.1.call-update) | async-done | bytes 7077904 | tf_op jit(solution)/shard_map/all_gather | solution.py:34
  81.1 5.2 fusion.26
  86.3 0.3 copy-done.1
  86.6 2.2 fusion.27
  88.8 2.2 fusion.28
  91.1 2.2 fusion.29
  93.3 2.6 fusion.5
  95.9 4.0 add_bitcast_fusion
  99.9 0.2 all-reduce.3.cloned.1.call-start
  100.2 0.5 copy-done.3
  100.7 6.3 %multiply_reduce_fusion.1 = (f32[128,192]{0,1:T(8,128)S(1)}, f32[128,64,192]{0,2,1:T(8,128)}) fusion(f32[128,64]{0,1:T(8,128)S(1)} %copy-done.5, bf16[192,128]{1,0:T(8,128)(2,1)S(1)} %copy-done.3, bf16[128,8192]{1,0:T(8,128)(2,1)S(1)} %copy-done), kind=kOutput, calls=%fused_computation.11 | convolution fusion | flops 416784384 | bytes 8568832 | tf_op jit(solution)/shard_map/tjd,sd->tjs/dot_general | solution.py:52
  107.1 70.3 %pmax.7 = f32[128]{0:T(128)S(1)} all-reduce(f32[128]{0:T(128)S(1)} %fusion.22), channel_id=1, replica_groups=mesh['row'=8,'col'=32] {'col'}, use_global_device_ids=true, to_apply=%region_2.3 | all-reduce | flops 128 | bytes 1024 | tf_op jit(solution)/shard_map/pmax | solution.py:57
  177.4 67.7 %psum.14 = f32[128]{0:T(128)S(1)} all-reduce(f32[128]{0:T(128)S(1)} %fusion.21), channel_id=1, replica_groups=mesh['row'=8,'col'=32] {'col'}, use_global_device_ids=true, to_apply=%region_4.5 | all-reduce | flops 128 | bytes 1024 | tf_op jit(solution)/shard_map/psum | solution.py:59
  245.2 5.3 %reduce-scatter.7.cloned.1.call-done = f32[192,128]{1,0:T(8,128)} async-done(((f32[6144,128]{1,0:T(8,128)}), f32[192,128]{1,0:T(8,128)}) %reduce-scatter.7.cloned.1.call-update) | async-done | bytes 98320
  250.4 0.9 fusion.20
  251.4 7.9 %multiply_reduce_fusion = (f32[128,64]{0,1:T(8,128)S(1)}, bf16[128,64,192]{0,2,1:T(8,128)(2,1)S(1)}) fusion(f32[128,192]{0,1:T(8,128)S(1)} %convert_element_type.16, f32[128,64,192]{0,2,1:T(8,128)} %get-tuple-element.18), kind=kLoop, calls=%fused_computation.9 | loop fusion | flops 22011904 | bytes 9568256 | tf_op jit(solution)/shard_map/reduce_sum | solution.py:74
  259.3 1.7 copy-done.2
  261.0 2.2 fusion.16
  263.2 4.6 fusion.23
  267.8 5.6 %copy.39 = f32[128,8192]{1,0:T(8,128)} copy(f32[128,8192]{0,1:T(8,128)} %bitcast.83) | data formatting | bytes 8388608 | tf_op jit(solution)/shard_map/reshape | solution.py:73
  273.7 0.5 copy-done.6
  274.2 0.6 dynamic-slice
  275.4 134.5 %all-reduce = f32[128,64]{0,1:T(8,128)S(1)} all-reduce(f32[128,64]{0,1:T(8,128)S(1)} %get-tuple-element.7), channel_id=4, replica_groups=mesh['row'=8,'col'=32] {'col'}, use_global_device_ids=true, to_apply=%region_17.18.clone | all-reduce | flops 8192 | bytes 65536
  409.9 0.6 constant_dynamic-slice_fusion
  410.4 1.5 broadcast_multiply_fusion
  412.0 102.4 %reduce-scatter.5.cloned.1.call-done = f32[128,256]{1,0:T(8,128)} async-done(((f32[128,8192]{1,0:T(8,128)}), f32[128,256]{1,0:T(8,128)}) %reduce-scatter.5.cloned.1.call-update) | async-done | bytes 131088 | tf_op jit(solution)/shard_map/reduce_scatter | solution.py:76
  514.4 0.2 mul.105
  514.6 1.6 bitcast_multiply_fusion
  (23 shorter events, 0.4 us)
Async XLA Ops:
  7.2 93.0 %copy-start = (bf16[128,8192]{1,0:T(8,128)(2,1)S(1)}, bf16[128,8192]{1,0:T(8,128)(2,1)}, u32[]{:S(2)}) copy-start(bf16[128,8192]{1,0:T(8,128)(2,1)} %param.9) | copy-start | bytes 6291460
  7.2 73.9 %all-gather.2.cloned.1.call-start = ((), (), s32[]{:S(2)}) async-start(), calls=%async_computation.2 | async-start | bytes 8110080 | tf_op jit(solution)/shard_map/all_gather | solution.py:34
  7.9 242.5 %reduce-scatter.7.cloned.1.call-start = ((), (), s32[]{:S(2)}) async-start(), calls=%async_computation.5 | async-start | bytes 3244032
  81.1 5.5 %copy-start.1 = (bf16[6144,576]{1,0:T(8,128)(2,1)S(1)}, bf16[6144,576]{1,0:T(8,128)(2,1)}, u32[]{:S(2)}) copy-start(bf16[6144,576]{1,0:T(8,128)(2,1)} %all-gather.2.cloned.1.call-done) | copy-start | bytes 21233668
  99.9 0.8 copy-start.3
  99.9 0.8 copy-start.5
  99.9 310.5 %all-reduce.3.cloned.1.call-start = ((), (), s32[]{:S(2)}) async-start(), calls=%async_computation.4 | async-start | bytes 196608 | tf_op jit(solution)/shard_map/psum | solution.py:68
  100.7 149.7 %copy-start.4 = (f32[128]{0:T(128)S(1)}, f32[128]{0:T(128)}, u32[]{:S(2)}) copy-start(f32[128]{0:T(128)} %param.13) | copy-start | bytes 1540
  259.3 1.7 copy-start.2
  263.2 251.2 %reduce-scatter.5.cloned.1.call-start = ((), (), s32[]{:S(2)}) async-start(), calls=%async_computation.3 | async-start | bytes 4325376 | tf_op jit(solution)/shard_map/reduce_scatter | solution.py:76
  273.5 0.7 copy-start.6
Sparse Core Ops, SparseCore 0:
  9.8 71.1 all-gather.1
  100.1 150.3 reduce-scatter.6
  263.3 92.9 all-reduce.2
  358.7 155.6 reduce-scatter.4
where the time goes:
time: 523 us
  blocking collectives  272 us (52%)
  waiting for transfers between devices  179 us (34%)
  matrix products  25.1 us (5%)
  other arithmetic  20.1 us (4%)
  between operations  14.5 us (3%)
  local copies, waits for them, and re-layouts  11.5 us (2%)
    unnamed x1, blocking collectives  134 us
    reduce_scatter x1, waiting for transfers between devices, body(): lax.psum_scatter(query_part, 'col', scatter_dimension=1, tiled=True)  102 us
    pmax x1, blocking collectives, body(): highest = lax.pmax(jnp.max(masked, axis=1), 'col')  70.3 us
    all_gather x1, waiting for transfers between devices, body(): keys_all = lax.all_gather(kv_latent, 'col', axis=0, tiled=True)  70.3 us
    psum x1, blocking collectives, body(): total = lax.psum(jnp.sum(raised, axis=1), 'col')  67.7 us
    dot_general x4, matrix products, body(): jnp.einsum('td,sd->ts', queries[:, head_index, :], keys_all, preferred_el...  11.9 us
  transfers between devices with their start and end apart: 4, of which 3 were waited for; matrix products, arithmetic and copies ran while one was open for 4% of the time, Pallas kernels for 0%

commit v1 on v0

--- a/solution.py
+++ b/solution.py
@@ -31,7 +31,8 @@
         rows_local, all_keys
     )
     allowed = (key_pos[None, :] <= query_pos[:, None]) & (expand > 0)
-    keys_all = lax.all_gather(kv_latent, "col", axis=0, tiled=True)
+    stack = jnp.stack([kv_latent] * lax.axis_size("col"))
+    keys_all = jnp.concatenate(lax.all_to_all(stack, "col", 0, 0), axis=0)
     queries = query_latent.reshape(rows_local, heads_local, latent)
     summed = jnp.zeros((rows_local, all_keys), jnp.float32)
     for head_index in range(heads_local):

time: 523 us -> 644 us (1.23)
  waiting for transfers between devices: 179 us -> 283 us
  starting transfers between devices: 0.34 us -> 9.3 us
    all_to_all x0 -> x1, waiting for transfers between devices: none -> 173 us  [body(): keys_all = jnp.concatenate(lax.all_to_all(stack, 'col', 0, 0), axis=0)]
    all_gather x1 -> x0, waiting for transfers between devices: 70.3 us -> none  [body(): keys_all = lax.all_gather(kv_latent, 'col', axis=0, tiled=True)]
    all_to_all x0 -> x1, starting transfers between devices: none -> 8.99 us  [body(): keys_all = jnp.concatenate(lax.all_to_all(stack, 'col', 0, 0), axis=0)]
  transfers between devices with their start and end apart: 4 -> 4, of which waited for: 3 -> 3; matrix products, arithmetic and copies ran while one was open for 4% -> 3% of each run, Pallas kernels for 0% -> 0%
where the time goes in v1:
time: 644 us; the launch traced here: 643 us
  waiting for transfers between devices  283 us (44%)
  blocking collectives  270 us (42%)
  matrix products  31.3 us (5%)
  other arithmetic  19.3 us (3%)
  local copies, waits for them, and re-layouts  15.4 us (2%)
  between operations  14.6 us (2%)
  starting transfers between devices  9.3 us (1%)
    all_to_all x1, waiting for transfers between devices, body(): keys_all = jnp.concatenate(lax.all_to_all(stack, 'col', 0, 0), axis=0)  173 us
    unnamed x1, blocking collectives  134 us
    reduce_scatter x1, waiting for transfers between devices, body(): lax.psum_scatter(query_part, 'col', scatter_dimension=1, tiled=True)  103 us
    psum x1, blocking collectives, body(): total = lax.psum(jnp.sum(raised, axis=1), 'col')  67.8 us
    pmax x1, blocking collectives, body(): highest = lax.pmax(jnp.max(masked, axis=1), 'col')  67.6 us
    dot_general x4, matrix products, body(): jnp.einsum('td,sd->ts', queries[:, head_index, :], keys_all, preferred_el...  18.1 us
  transfers between devices with their start and end apart: 4, of which 3 were waited for; matrix products, arithmetic and copies ran while one was open for 3% of the time, Pallas kernels for 0%

profile of v1, /device:TPU:16, one launch (start us, length us, event | category | flops | bytes accessed | tf_op | source)
XLA Modules:
  0.0 642.8 jit_solution(14419429402350960341)
XLA Ops:
  7.2 5.3 stack.2
  12.5 9.0 %all-to-all-start = ((bf16[32,192,576]{2,1,0:T(8,128)(2,1)}), bf16[32,192,576]{2,1,0:T(8,128)(2,1)}, u32[]{:S(2)}, u32[]{:S(2)}) async-start(bf16[32,192,576]{2,1,0:T(8,128)(2,1)} %stack.2), calls=%async_computation | async-start | bytes 15728640 | tf_op jit(solution)/shard_map/all_to_all | solution.py:35
  21.6 0.3 copy.32
  21.9 0.6 fusion.4
  22.6 172.9 %all-to-all-done = bf16[32,192,576]{2,1,0:T(8,128)(2,1)} async-done(((bf16[32,192,576]{2,1,0:T(8,128)(2,1)}), bf16[32,192,576]{2,1,0:T(8,128)(2,1)}, u32[]{:S(2)}, u32[]{:S(2)}) %all-to-all-start) | async-done | bytes 7077920 | tf_op jit(solution)/shard_map/all_to_all | solution.py:35
  195.4 4.5 fusion.26
  200.0 4.5 fusion.27
  204.5 4.5 fusion.28
  209.1 4.5 fusion.29
  213.6 2.6 fusion.5
  216.2 4.0 add_bitcast_fusion
  220.2 0.2 all-reduce.3.cloned.1.call-start
  220.5 0.5 copy-done.3
  221.0 6.3 multiply_reduce_fusion.1
  227.4 67.6 %pmax.7 = f32[128]{0:T(128)S(1)} all-reduce(f32[128]{0:T(128)S(1)} %fusion.22), channel_id=1, replica_groups=mesh['row'=8,'col'=32] {'col'}, use_global_device_ids=true, to_apply=%region_2.3 | all-reduce | flops 128 | bytes 1024 | tf_op jit(solution)/shard_map/pmax | solution.py:58
  295.0 67.8 %psum.14 = f32[128]{0:T(128)S(1)} all-reduce(f32[128]{0:T(128)S(1)} %fusion.21), channel_id=1, replica_groups=mesh['row'=8,'col'=32] {'col'}, use_global_device_ids=true, to_apply=%region_4.5 | all-reduce | flops 128 | bytes 1024 | tf_op jit(solution)/shard_map/psum | solution.py:60
  362.8 7.0 %reduce-scatter.7.cloned.1.call-done = f32[192,128]{1,0:T(8,128)} async-done(((f32[6144,128]{1,0:T(8,128)}), f32[192,128]{1,0:T(8,128)}) %reduce-scatter.7.cloned.1.call-update) | async-done | bytes 98320
  369.9 0.9 fusion.20
  370.8 7.9 %multiply_reduce_fusion = (f32[128,64]{0,1:T(8,128)S(1)}, bf16[128,64,192]{0,2,1:T(8,128)(2,1)S(1)}) fusion(f32[128,192]{0,1:T(8,128)S(1)} %convert_element_type.16, f32[128,64,192]{0,2,1:T(8,128)} %get-tuple-element.18), kind=kLoop, calls=%fused_computation.9 | loop fusion | flops 22011904 | bytes 9568256 | tf_op jit(solution)/shard_map/reduce_sum | solution.py:75
  378.7 1.7 copy-done.1
  380.4 2.2 fusion.16
  382.7 4.6 fusion.23
  387.3 5.6 copy.39
  393.0 0.1 copy.40
  393.1 0.5 copy-done.7
  393.6 0.6 dynamic-slice
  394.8 134.2 %all-reduce = f32[128,64]{0,1:T(8,128)S(1)} all-reduce(f32[128,64]{0,1:T(8,128)S(1)} %get-tuple-element.7), channel_id=4, replica_groups=mesh['row'=8,'col'=32] {'col'}, use_global_device_ids=true, to_apply=%region_17.18.clone | all-reduce | flops 8192 | bytes 65536
  529.0 0.6 constant_dynamic-slice_fusion
  529.6 1.5 broadcast_multiply_fusion
  531.1 103.3 %reduce-scatter.5.cloned.1.call-done = f32[128,256]{1,0:T(8,128)} async-done(((f32[128,8192]{1,0:T(8,128)}), f32[128,256]{1,0:T(8,128)}) %reduce-scatter.5.cloned.1.call-update) | async-done | bytes 131088 | tf_op jit(solution)/shard_map/reduce_scatter | solution.py:77
  634.5 0.2 mul.105
  634.7 1.6 bitcast_multiply_fusion
  (25 shorter events, 0.3 us)
Async XLA Ops:
  7.2 213.3 %copy-start = (bf16[128,8192]{1,0:T(8,128)(2,1)S(1)}, bf16[128,8192]{1,0:T(8,128)(2,1)}, u32[]{:S(2)}) copy-start(bf16[128,8192]{1,0:T(8,128)(2,1)} %param.9) | copy-start | bytes 6291460
  12.5 9.1 %copy-start.2 = (bf16[128,2304]{1,0:T(8,128)(2,1)S(1)}, bf16[128,2304]{1,0:T(8,128)(2,1)}, u32[]{:S(2)}) copy-start(bf16[128,2304]{1,0:T(8,128)(2,1)} %param.7) | copy-start | bytes 1769476
  12.5 9.4 %copy-start.4 = (s32[128,96]{0,1:T(8,128)S(1)}, s32[128,96]{0,1:T(8,128)}, u32[]{:S(2)}) copy-start(s32[128,96]{0,1:T(8,128)} %param.12) | copy-start | bytes 147460
  12.5 182.9 %all-to-all-start = ((bf16[32,192,576]{2,1,0:T(8,128)(2,1)}), bf16[32,192,576]{2,1,0:T(8,128)(2,1)}, u32[]{:S(2)}, u32[]{:S(2)}) async-start(bf16[32,192,576]{2,1,0:T(8,128)(2,1)} %stack.2), calls=%async_computation | async-start | bytes 15728640 | tf_op jit(solution)/shard_map/all_to_all | solution.py:35
  21.5 348.4 %reduce-scatter.7.cloned.1.call-start = ((), (), s32[]{:S(2)}) async-start(), calls=%async_computation.5 | async-start | bytes 3244032
  220.2 0.8 copy-start.3
  220.2 0.8 copy-start.6
  220.2 309.3 %all-reduce.3.cloned.1.call-start = ((), (), s32[]{:S(2)}) async-start(), calls=%async_computation.4 | async-start | bytes 196608 | tf_op jit(solution)/shard_map/psum | solution.py:69
  221.0 148.9 %copy-start.5 = (f32[128]{0:T(128)S(1)}, f32[128]{0:T(128)}, u32[]{:S(2)}) copy-start(f32[128]{0:T(128)} %param.13) | copy-start | bytes 1540
  378.7 1.7 copy-start.1
  382.6 251.8 %reduce-scatter.5.cloned.1.call-start = ((), (), s32[]{:S(2)}) async-start(), calls=%async_computation.3 | async-start | bytes 4325376 | tf_op jit(solution)/shard_map/reduce_scatter | solution.py:77
  392.9 0.7 copy-start.7
Sparse Core Ops, SparseCore 0:
  220.4 149.4 reduce-scatter.6
  382.7 93.6 all-reduce.2
  479.0 155.4 reduce-scatter.4
